TPU v7x, 32 devices: a whole 2x2x4 slice. The times are simulated.
32 devices in a mesh: expert: 16 (over z, y, x), replica: 2 (over core).
Axes of the slice: x: 2, y: 2, z: 4, core: 2. Of those that a mesh axis runs over, the one named last changes fastest.
Arguments:
- tokens: bfloat16 [1024, 7168], P('expert', 'replica'), may hold values from -6 to 6
- routes: int32 [1024, 8], P('expert'), may hold values from 0 to 15, all different within a row; in each aligned block of 64 rows (0 to 63, 64 to 127, ...) at most 64 rows name the same one
- route_scores: float32 [1024, 8], P('expert'), may hold values from 0.05 to 1
- placement: int32 [16], replicated, may hold values from 0 to 15, each once
- w_in: bfloat16 [16, 7168, 2, 1024], P('expert', 'replica'), may hold values from -0.0625 to 0.0625
- w_out: bfloat16 [16, 1024, 7168], P('expert', None, 'replica'), may hold values from -0.1875 to 0.1875
Outputs:
- mixed: bfloat16 [1024, 7168], P('expert', 'replica')
Inputs may be any that keep to these rules, and one draw needn't show every extreme that they name: `routes`: each row names 8 different logical experts. Among the 64 rows of each aligned block (the tokens of one index of the expert axis) no expert is named by more than 64 rows, a bound that some block reaches. `placement`: A permutation of the physical slots.
All inputs are finite; a program needn't handle non-finite values.
Results may differ from a plain program's by a relative error of at most 0.0057.
Values may be sent and summed in bfloat16 or wider, within the bound.
A program may use at most 128 MiB of HBM per device.

v0:
```python
import jax
import jax.numpy as jnp
from jax import lax
from jax.sharding import PartitionSpec as P


def packed(tokens, routes, route_scores, placement, w_in, w_out):
    tok_rows, feature_cols = tokens.shape
    route_count = routes.shape[1]
    experts = placement.shape[0]
    hidden_units = w_in.shape[3]
    capacity = min(tok_rows, max(2, 2 * tok_rows * route_count // experts))
    slot_total = experts * capacity
    expert_ids = jnp.arange(experts, dtype=jnp.int32)
    route_table = routes[:, :, None] == expert_ids
    physical = jnp.sum(jnp.where(route_table, placement, 0), axis=-1)
    flat_slots = physical.reshape(-1)
    onehot = (flat_slots[:, None] == expert_ids).astype(jnp.int32)
    earlier = jnp.sum((jnp.cumsum(onehot, axis=0) - onehot) * onehot, axis=1)
    position = (flat_slots * capacity + earlier).reshape(tok_rows, route_count)
    slot_index = jnp.arange(slot_total, dtype=jnp.int32)
    placing = jnp.any(position[None, :, :] == slot_index[:, None, None], axis=-1).astype(
        jnp.bfloat16
    )
    outgoing = jnp.dot(placing, tokens, preferred_element_type=jnp.float32).astype(jnp.bfloat16)
    incoming = lax.all_to_all(outgoing, "expert", split_axis=0, concat_axis=0, tiled=True)
    weights_in = w_in[0].reshape(feature_cols, 2 * hidden_units)
    weights_out = w_out[0]
    partial_value = jnp.dot(incoming, weights_in, preferred_element_type=jnp.float32)
    partial_value = partial_value.reshape(slot_total, 2, hidden_units)
    shares = lax.psum_scatter(partial_value, "replica", scatter_dimension=2, tiled=True)
    active = (jax.nn.silu(shares[:, 0]) * shares[:, 1]).astype(jnp.bfloat16)
    result = jnp.dot(
        lax.all_gather(active, "replica", axis=1, tiled=True),
        weights_out,
        preferred_element_type=jnp.float32,
    )
    expert_out = result.astype(jnp.bfloat16)
    returned = lax.all_to_all(expert_out, "expert", split_axis=0, concat_axis=0, tiled=True)
    route_weight = 2.5 * route_scores / jnp.sum(route_scores, axis=1, keepdims=True)
    picked = returned[position.reshape(-1)].reshape(tok_rows, route_count, feature_cols)
    mixed = jnp.sum(picked.astype(jnp.float32) * route_weight[:, :, None], axis=1)
    return mixed.astype(jnp.bfloat16)


def expert_weights(routes, route_scores, placement):
    experts = placement.shape[0]
    expert_ids = jnp.arange(experts, dtype=jnp.int32)
    physical = jnp.sum(jnp.where(routes[:, :, None] == expert_ids, placement, 0), axis=-1)
    route_weight = 2.5 * route_scores / jnp.sum(route_scores, axis=1, keepdims=True)
    return jnp.sum(
        jnp.where(physical[:, :, None] == expert_ids, route_weight[:, :, None], 0.0), axis=1
    )


def dense(tokens, routes, route_scores, placement, w_in, w_out):
    feature_cols = tokens.shape[1]
    hidden_units = w_in.shape[3]
    table = expert_weights(routes, route_scores, placement)
    mine = lax.all_to_all(table, "expert", split_axis=1, concat_axis=0, tiled=True)
    incoming = lax.all_gather(tokens, "expert", axis=0, tiled=True)
    rows = incoming.shape[0]
    weights_in = w_in[0].reshape(feature_cols, 2 * hidden_units)
    partial_value = jnp.dot(incoming, weights_in, preferred_element_type=jnp.float32)
    partial_value = partial_value.reshape(rows, 2, hidden_units)
    shares = lax.psum_scatter(partial_value, "replica", scatter_dimension=2, tiled=True)
    active = (jax.nn.silu(shares[:, 0]) * shares[:, 1]).astype(jnp.bfloat16)
    result = jnp.dot(
        lax.all_gather(active, "replica", axis=1, tiled=True),
        w_out[0],
        preferred_element_type=jnp.float32,
    )
    weighted = (result.astype(jnp.bfloat16).astype(jnp.float32) * mine).astype(jnp.bfloat16)
    return lax.psum_scatter(weighted, "expert", scatter_dimension=0, tiled=True)


def on_device(tokens, routes, route_scores, placement, w_in, w_out):
    tok_rows = tokens.shape[0]
    if 2 * tok_rows * routes.shape[1] // placement.shape[0] >= tok_rows:
        return dense(tokens, routes, route_scores, placement, w_in, w_out)
    return packed(tokens, routes, route_scores, placement, w_in, w_out)


def solution(mesh):
    in_specs = (
        P("expert", "replica"),
        P("expert", None),
        P("expert", None),
        P(),
        P("expert", "replica", None, None),
        P("expert", None, "replica"),
    )
    out_specs = P("expert", "replica")
    return jax.shard_map(
        on_device, mesh=mesh, in_specs=in_specs, out_specs=out_specs, check_vma=False
    )
```

profile of v0, /device:TPU:10, one launch (start us, length us, event | category | flops | bytes accessed | tf_op | source)
XLA Modules:
  0.0 345.8 jit_solution(17655661760736529164)
XLA Ops:
  6.5 0.0 all-gather.3.cloned.1.call-start
  6.5 0.7 all-gather.3.cloned.1.call-update
  7.3 0.0 reduce-scatter.3.cloned.1.call-start
  7.3 16.1 %copy.18 = bf16[448,8,2,1024]{3,1,2,0:T(8,128)(2,1)} copy(bf16[448,8,2,1024]{3,2,1,0:T(2,128)(2,1)} %bitcast.32) | data formatting | bytes 29360128
  23.4 18.9 %copy.16 = bf16[2048,3584]{1,0:T(8,128)(2,1)} copy(bf16[2048,3584]{0,1:T(8,128)(2,1)} %bitcast.31) | data formatting | bytes 29360128 | tf_op jit(solution)/shard_map/dot_general | solution.py:64
  42.3 71.1 %all-gather.3.cloned.1.call-done = bf16[1024,3584]{1,0:T(8,128)(2,1)} async-done(((bf16[64,3584]{1,0:T(8,128)(2,1)}), bf16[1024,3584]{1,0:T(8,128)(2,1)}) %all-gather.3.cloned.1.call-update) | async-done | bytes 7340048 | tf_op jit(solution)/shard_map/all_gather | solution.py:61
  113.4 21.6 %fusion.3 = f32[1024,2,1024]{2,0,1:T(8,128)} fusion(bf16[2,1024,3584]{2,1,0:T(8,128)(2,1)} %bitcast.33, bf16[1024,3584]{1,0:T(8,128)(2,1)} %all-gather.3.cloned.1.call-done), kind=kOutput, calls=%fused_computation.3 | convolution fusion | flops 15032385536 | bytes 30408704 | tf_op jit(solution)/shard_map/dot_general | solution.py:64
  135.0 0.0 copy-start
  135.0 0.0 copy-start.1
  135.0 0.0 copy-start.2
  135.0 0.0 reduce-scatter.3.cloned.1.call-update
  135.0 0.0 all-gather.5.cloned.1.call-start
  135.0 15.7 %reduce-scatter.3.cloned.1.call-done = f32[1024,2,512]{2,0,1:T(8,128)} async-done(((f32[1024,2,1024]{2,0,1:T(8,128)}), f32[1024,2,512]{2,0,1:T(8,128)}) %reduce-scatter.3.cloned.1.call-update) | async-done | bytes 4194320 | tf_op jit(solution)/shard_map/reduce_scatter | solution.py:66
  150.7 3.8 %fusion.6 = bf16[1024,512]{1,0:T(8,128)(2,1)} fusion(f32[1024,2,512]{2,0,1:T(8,128)} %reduce-scatter.3.cloned.1.call-done), kind=kLoop, calls=%fused_computation.7 | loop fusion | flops 3145728 | bytes 5242880 | tf_op jit(solution)/shard_map/convert_element_type | solution.py:67
  154.5 0.0 all-gather.5.cloned.1.call-update
  154.6 0.0 reduce-scatter.5.cloned.1.call-start
  154.6 0.0 copy-done
  154.7 0.0 copy-done.1
  154.7 0.0 copy-done.2
  154.7 0.1 select_reduce_fusion.1
  154.8 11.8 %all_to_all.16 = f32[64,16,1]{0,2,1:T(1,128)S(1)} all-to-all(f32[64,16,1]{0,2,1:T(1,128)S(1)} %bitcast.34), channel_id=1, replica_groups=mesh['expert'=16,'replica'=2] {'expert'}, dimensions={1} | all-to-all | bytes 8192 | tf_op jit(solution)/shard_map/all_to_all | solution.py:60
  166.7 0.1 mul.27
  166.7 0.0 all-gather.5.cloned.1.call-done
  166.7 12.5 %multiply_convert_fusion = bf16[1024,3584]{1,0:T(8,128)(2,1)} fusion(bf16[1024,1024]{1,0:T(8,128)(2,1)} %all-gather.5.cloned.1.call-done, bf16[1,1024,3584]{2,1,0:T(8,128)(2,1)} %param.11, f32[1024]{0:T(1024)S(1)} %mul.27), kind=kOutput, calls=%fused_computation | convolution fusion | flops 7530872832 | bytes 16781312 | tf_op jit(solution)/shard_map/dot_general | solution.py:68
  179.2 0.0 reduce-scatter.5.cloned.1.call-update
  179.3 160.0 %reduce-scatter.5.cloned.1.call-done = bf16[64,3584]{1,0:T(8,128)(2,1)} async-done(((bf16[1024,3584]{1,0:T(8,128)(2,1)}), bf16[64,3584]{1,0:T(8,128)(2,1)}) %reduce-scatter.5.cloned.1.call-update) | async-done | bytes 458768 | tf_op jit(solution)/shard_map/reduce_scatter | solution.py:74
  (4 shorter events, 0.1 us)
Async XLA Ops:
  6.5 106.8 %all-gather.3.cloned.1.call-start = ((), (), s32[]{:S(2)}) async-start(), calls=%async_computation.3 | async-start | bytes 7798784 | tf_op jit(solution)/shard_map/all_gather | solution.py:61
  7.3 143.4 %reduce-scatter.3.cloned.1.call-start = ((), (), s32[]{:S(2)}) async-start(), calls=%async_computation.4 | async-start | bytes 12582912 | tf_op jit(solution)/shard_map/reduce_scatter | solution.py:66
  135.0 19.7 %copy-start = (f32[64,8]{0,1:T(8,128)S(1)}, f32[64,8]{0,1:T(8,128)}, u32[]{:S(2)}) copy-start(f32[64,8]{0,1:T(8,128)} %param.8) | copy-start | bytes 6148
  135.0 19.7 %copy-start.1 = (s32[64,8]{0,1:T(8,128)S(1)}, s32[64,8]{0,1:T(8,128)}, u32[]{:S(2)}) copy-start(s32[64,8]{0,1:T(8,128)} %param.7) | copy-start | bytes 6148
  135.0 19.7 %copy-start.2 = (s32[16]{0:T(128)S(1)}, s32[16]{0:T(128)}, u32[]{:S(2)}) copy-start(s32[16]{0:T(128)} %param.9) | copy-start | bytes 196
  135.0 31.7 %all-gather.5.cloned.1.call-start = ((), (), s32[]{:S(2)}) async-start(), calls=%async_computation.5 | async-start | bytes 3145728 | tf_op jit(solution)/shard_map/all_gather | solution.py:69
  154.6 184.7 %reduce-scatter.5.cloned.1.call-start = ((), (), s32[]{:S(2)}) async-start(), calls=%async_computation.6 | async-start | bytes 7798784 | tf_op jit(solution)/shard_map/reduce_scatter | solution.py:74
Sparse Core Ops, SparseCore 0:
  10.0 103.2 all-gather.2
  135.1 15.5 reduce-scatter.2
  154.7 11.7 all-gather.4
  179.4 159.8 reduce-scatter.4
where the time goes:
time: 347 us; the launch traced here: 346 us
  waiting for transfers between devices  248 us (71%)
  local copies, waits for them, and re-layouts  35.1 us (10%)
  matrix products  34.1 us (10%)
  between operations  13.2 us (4%)
  blocking collectives  11.8 us (3%)
  other arithmetic  3.98 us (1%)
    reduce_scatter x1, waiting for transfers between devices, dense(): return lax.psum_scatter(weighted, 'expert', scatter_dimension=0, tiled=True)  160 us
    all_gather x1, waiting for transfers between devices, dense(): incoming = lax.all_gather(tokens, 'expert', axis=0, tiled=True)  71.1 us
    dot_general x1, matrix products, dense(): jnp.dot(incoming, weights_in, preferred_element_type=jnp.float32)  21.6 us
    dot_general x1, local copies, waits for them, and re-layouts, dense(): jnp.dot(incoming, weights_in, preferred_element_type=jnp.float32)  18.9 us
    unnamed x7, local copies, waits for them, and re-layouts  16.1 us
    reduce_scatter x1, waiting for transfers between devices, dense(): lax.psum_scatter(partial_value, 'replica', scatter_dimension=2, tiled=True)  15.7 us
    dot_general x1, matrix products, dense(): jnp.dot(lax.all_gather(active, 'replica', axis=1, tiled=True), w_out[0],...  12.5 us
    all_to_all x1, blocking collectives, dense(): lax.all_to_all(table, 'expert', split_axis=1, concat_axis=0, tiled=True)  11.8 us
  transfers between devices with their start and end apart: 4, of which 3 were waited for; matrix products, arithmetic and copies ran while one was open for 10% of the time, Pallas kernels for 0%

commit v1 on v0

--- a/solution.py
+++ b/solution.py
@@ -58,7 +58,14 @@
     hidden_units = w_in.shape[3]
     table = expert_weights(routes, route_scores, placement)
     mine = lax.all_to_all(table, "expert", split_axis=1, concat_axis=0, tiled=True)
-    incoming = lax.all_gather(tokens, "expert", axis=0, tiled=True)
+    ring = [tokens]
+    for hop in range(15):
+        ring.append(lax.ppermute(ring[-1], "expert", [(dev, (dev + 1) % 16) for dev in range(16)]))
+    incoming = jnp.roll(
+        jnp.concatenate(ring[::-1], axis=0),
+        (lax.axis_index("expert") + 1) * ring[0].shape[0],
+        axis=0,
+    )
     rows = incoming.shape[0]
     weights_in = w_in[0].reshape(feature_cols, 2 * hidden_units)
     partial_value = jnp.dot(incoming, weights_in, preferred_element_type=jnp.float32)

time: 347 us -> 503 us (1.45)
  waiting for transfers between devices: 248 us -> 369 us
  local copies, waits for them, and re-layouts: 35.1 us -> 61.4 us
  starting transfers between devices: 0.12 us -> 10.5 us
    ppermute x0 -> x15, waiting for transfers between devices: none -> 168 us  [dense(): lax.ppermute(ring[-1], 'expert', [(dev, (dev + 1) % 16) for dev in range(...]
    all_gather x1 -> x0, waiting for transfers between devices: 71.1 us -> none  [dense(): incoming = lax.all_gather(tokens, 'expert', axis=0, tiled=True)]
    unnamed x7 -> x68, local copies, waits for them, and re-layouts: 16.1 us -> 42.5 us
    reduce_scatter x1, waiting for transfers between devices: 15.7 us -> 41.1 us  [dense(): lax.psum_scatter(partial_value, 'replica', scatter_dimension=2, tiled=True)]
    ppermute x0 -> x15, starting transfers between devices: none -> 10.4 us  [dense(): lax.ppermute(ring[-1], 'expert', [(dev, (dev + 1) % 16) for dev in range(...]
  transfers between devices with their start and end apart: 4 -> 18, of which waited for: 3 -> 16; matrix products, arithmetic and copies ran while one was open for 10% -> 7% of each run, Pallas kernels for 0% -> 0%
where the time goes in v1:
time: 503 us; the launch traced here: 502 us
  waiting for transfers between devices  369 us (73%)
  local copies, waits for them, and re-layouts  61.4 us (12%)
  matrix products  31.8 us (6%)
  between operations  13.5 us (3%)
  blocking collectives  11.8 us (2%)
  starting transfers between devices  10.5 us (2%)
    ppermute x15, waiting for transfers between devices, dense(): lax.ppermute(ring[-1], 'expert', [(dev, (dev + 1) % 16) for dev in range(...  168 us
    reduce_scatter x1, waiting for transfers between devices, dense(): return lax.psum_scatter(weighted, 'expert', scatter_dimension=0, tiled=True)  160 us
    unnamed x68, local copies, waits for them, and re-layouts  42.5 us
    reduce_scatter x1, waiting for transfers between devices, dense(): lax.psum_scatter(partial_value, 'replica', scatter_dimension=2, tiled=True)  41.1 us
    dot_general x1, matrix products, dense(): jnp.dot(incoming, weights_in, preferred_element_type=jnp.float32)  19.3 us
    dot_general x1, local copies, waits for them, and re-layouts, dense(): jnp.dot(incoming, weights_in, preferred_element_type=jnp.float32)  18.8 us
    dot_general x1, matrix products, dense(): jnp.dot(lax.all_gather(active, 'replica', axis=1, tiled=True), w_out[0],...  12.5 us
    all_to_all x1, blocking collectives, dense(): lax.all_to_all(table, 'expert', split_axis=1, concat_axis=0, tiled=True)  11.8 us
  transfers between devices with their start and end apart: 18, of which 16 were waited for; matrix products, arithmetic and copies ran while one was open for 7% of the time, Pallas kernels for 0%

profile of v1, /device:TPU:10, one launch (start us, length us, event | category | flops | bytes accessed | tf_op | source)
XLA Modules:
  0.0 501.8 jit_solution(6012919315221202801)
XLA Ops:
  6.5 1.5 collective-permute-start
  8.0 11.0 %collective-permute-done = bf16[64,3584]{1,0:T(8,128)(2,1)S(1)} collective-permute-done((bf16[64,3584]{1,0:T(8,128)(2,1)}, bf16[64,3584]{1,0:T(8,128)(2,1)S(1)}, u32[]{:S(2)}, u32[]{:S(2)}) %collective-permute-start) | collective-permute-done | bytes 458784 | tf_op jit(solution)/shard_map/ppermute | solution.py:63
  19.0 2.4 collective-permute-start.1
  21.4 9.6 %collective-permute-done.1 = bf16[64,3584]{1,0:T(8,128)(2,1)S(1)} collective-permute-done((bf16[64,3584]{1,0:T(8,128)(2,1)S(1)}, bf16[64,3584]{1,0:T(8,128)(2,1)S(1)}, u32[]{:S(2)}, u32[]{:S(2)}) %collective-permute-start.1) | collective-permute-done | bytes 458784 | tf_op jit(solution)/shard_map/ppermute | solution.py:63
  31.0 2.7 collective-permute-start.2
  33.7 9.6 %collective-permute-done.2 = bf16[64,3584]{1,0:T(8,128)(2,1)S(1)} collective-permute-done((bf16[64,3584]{1,0:T(8,128)(2,1)S(1)}, bf16[64,3584]{1,0:T(8,128)(2,1)S(1)}, u32[]{:S(2)}, u32[]{:S(2)}) %collective-permute-start.2) | collective-permute-done | bytes 458784 | tf_op jit(solution)/shard_map/ppermute | solution.py:63
  43.3 1.8 collective-permute-start.3
  45.1 9.7 %collective-permute-done.3 = bf16[64,3584]{1,0:T(8,128)(2,1)S(1)} collective-permute-done((bf16[64,3584]{1,0:T(8,128)(2,1)S(1)}, bf16[64,3584]{1,0:T(8,128)(2,1)S(1)}, u32[]{:S(2)}, u32[]{:S(2)}) %collective-permute-start.3) | collective-permute-done | bytes 458784 | tf_op jit(solution)/shard_map/ppermute | solution.py:63
  54.8 1.0 collective-permute-start.4
  55.8 9.7 %collective-permute-done.4 = bf16[64,3584]{1,0:T(8,128)(2,1)S(1)} collective-permute-done((bf16[64,3584]{1,0:T(8,128)(2,1)S(1)}, bf16[64,3584]{1,0:T(8,128)(2,1)S(1)}, u32[]{:S(2)}, u32[]{:S(2)}) %collective-permute-start.4) | collective-permute-done | bytes 458784 | tf_op jit(solution)/shard_map/ppermute | solution.py:63
  66.1 10.4 %collective-permute-done.5 = bf16[64,3584]{1,0:T(8,128)(2,1)S(1)} collective-permute-done((bf16[64,3584]{1,0:T(8,128)(2,1)S(1)}, bf16[64,3584]{1,0:T(8,128)(2,1)S(1)}, u32[]{:S(2)}, u32[]{:S(2)}) %collective-permute-start.5) | collective-permute-done | bytes 458784 | tf_op jit(solution)/shard_map/ppermute | solution.py:63
  76.9 11.4 %collective-permute-done.6 = bf16[64,3584]{1,0:T(8,128)(2,1)S(1)} collective-permute-done((bf16[64,3584]{1,0:T(8,128)(2,1)S(1)}, bf16[64,3584]{1,0:T(8,128)(2,1)S(1)}, u32[]{:S(2)}, u32[]{:S(2)}) %collective-permute-start.6) | collective-permute-done | bytes 458784 | tf_op jit(solution)/shard_map/ppermute | solution.py:63
  88.2 0.8 copy-done.2
  89.1 13.0 %collective-permute-done.7 = bf16[64,3584]{1,0:T(8,128)(2,1)S(1)} collective-permute-done((bf16[64,3584]{1,0:T(8,128)(2,1)S(1)}, bf16[64,3584]{1,0:T(8,128)(2,1)S(1)}, u32[]{:S(2)}, u32[]{:S(2)}) %collective-permute-start.7) | collective-permute-done | bytes 458784 | tf_op jit(solution)/shard_map/ppermute | solution.py:63
  102.0 0.8 copy-done.4
  102.8 14.1 %collective-permute-done.8 = bf16[64,3584]{1,0:T(8,128)(2,1)S(1)} collective-permute-done((bf16[64,3584]{1,0:T(8,128)(2,1)S(1)}, bf16[64,3584]{1,0:T(8,128)(2,1)S(1)}, u32[]{:S(2)}, u32[]{:S(2)}) %collective-permute-start.8) | collective-permute-done | bytes 458784 | tf_op jit(solution)/shard_map/ppermute | solution.py:63
  117.0 0.8 copy-done.6
  117.7 15.3 %collective-permute-done.9 = bf16[64,3584]{1,0:T(8,128)(2,1)S(1)} collective-permute-done((bf16[64,3584]{1,0:T(8,128)(2,1)S(1)}, bf16[64,3584]{1,0:T(8,128)(2,1)S(1)}, u32[]{:S(2)}, u32[]{:S(2)}) %collective-permute-start.9) | collective-permute-done | bytes 458784 | tf_op jit(solution)/shard_map/ppermute | solution.py:63
  133.1 0.8 copy-done.8
  133.8 14.6 %collective-permute-done.10 = bf16[64,3584]{1,0:T(8,128)(2,1)S(1)} collective-permute-done((bf16[64,3584]{1,0:T(8,128)(2,1)S(1)}, bf16[64,3584]{1,0:T(8,128)(2,1)S(1)}, u32[]{:S(2)}, u32[]{:S(2)}) %collective-permute-start.10) | collective-permute-done | bytes 458784 | tf_op jit(solution)/shard_map/ppermute | solution.py:63
  148.4 0.8 copy-done.10
  149.2 13.4 %collective-permute-done.11 = bf16[64,3584]{1,0:T(8,128)(2,1)S(1)} collective-permute-done((bf16[64,3584]{1,0:T(8,128)(2,1)S(1)}, bf16[64,3584]{1,0:T(8,128)(2,1)S(1)}, u32[]{:S(2)}, u32[]{:S(2)}) %collective-permute-start.11) | collective-permute-done | bytes 458784 | tf_op jit(solution)/shard_map/ppermute | solution.py:63
  162.6 0.8 copy-done.12
  163.4 12.5 %collective-permute-done.12 = bf16[64,3584]{1,0:T(8,128)(2,1)S(1)} collective-permute-done((bf16[64,3584]{1,0:T(8,128)(2,1)S(1)}, bf16[64,3584]{1,0:T(8,128)(2,1)S(1)}, u32[]{:S(2)}, u32[]{:S(2)}) %collective-permute-start.12) | collective-permute-done | bytes 458784 | tf_op jit(solution)/shard_map/ppermute | solution.py:63
  175.9 0.8 copy-done.13
  176.7 13.4 %collective-permute-done.13 = bf16[64,3584]{1,0:T(8,128)(2,1)} collective-permute-done((bf16[64,3584]{1,0:T(8,128)(2,1)S(1)}, bf16[64,3584]{1,0:T(8,128)(2,1)}, u32[]{:S(2)}, u32[]{:S(2)}) %collective-permute-start.13) | collective-permute-done | bytes 458784 | tf_op jit(solution)/shard_map/ppermute | solution.py:63
  190.0 16.1 %copy.18 = bf16[448,8,2,1024]{3,1,2,0:T(8,128)(2,1)} copy(bf16[448,8,2,1024]{3,2,1,0:T(2,128)(2,1)} %bitcast.32) | data formatting | bytes 29360128
  206.1 18.8 %copy.16 = bf16[2048,3584]{1,0:T(8,128)(2,1)} copy(bf16[2048,3584]{0,1:T(8,128)(2,1)} %bitcast.31) | data formatting | bytes 29360128 | tf_op jit(solution)/shard_map/dot_general | solution.py:71
  224.9 1.2 constant_dynamic-update-slice_fusion.31
  226.1 1.7 constant_dynamic-update-slice_fusion.30
  227.9 1.4 constant_dynamic-update-slice_fusion.29
  229.3 1.4 constant_dynamic-update-slice_fusion.28
  230.7 1.1 constant_dynamic-update-slice_fusion.27
  231.8 1.1 constant_dynamic-update-slice_fusion.26
  232.8 1.1 constant_dynamic-update-slice_fusion.25
  233.9 1.1 constant_dynamic-update-slice_fusion.24
  234.9 1.1 constant_dynamic-update-slice_fusion.23
  236.3 1.1 constant_dynamic-update-slice_fusion.15
  237.3 1.1 constant_dynamic-update-slice_fusion.14
  238.4 1.1 constant_dynamic-update-slice_fusion.13
  239.4 1.1 constant_dynamic-update-slice_fusion.12
  241.0 5.1 %copy-done.15 = bf16[2048,3584]{1,0:T(8,128)(2,1)} copy-done((bf16[2048,3584]{1,0:T(8,128)(2,1)}, bf16[2048,3584]{1,0:T(8,128)(2,1)S(1)}, u32[]{:S(2)}) %copy-start.15) | copy-done | bytes 14680088
  246.2 19.3 %fusion.3 = f32[1024,2,1024]{2,0,1:T(8,128)} fusion(bf16[2,1024,3584]{2,1,0:T(8,128)(2,1)S(1)} %bitcast.33, bf16[2048,3584]{1,0:T(8,128)(2,1)} %copy-done.15, s32[]{:T(128)S(6)} %select_n.22), kind=kOutput, calls=%fused_computation.3 | convolution fusion | flops 15032385536 | bytes 30408708 | tf_op jit(solution)/shard_map/dot_general | solution.py:71
  265.5 41.1 %reduce-scatter.3.cloned.1.call-done = f32[1024,2,512]{2,0,1:T(8,128)} async-done(((f32[1024,2,1024]{2,0,1:T(8,128)}), f32[1024,2,512]{2,0,1:T(8,128)}) %reduce-scatter.3.cloned.1.call-update) | async-done | bytes 4194320 | tf_op jit(solution)/shard_map/reduce_scatter | solution.py:73
  306.6 3.9 fusion.7
  310.7 11.8 %all_to_all.16 = f32[64,16,1]{0,2,1:T(1,128)S(1)} all-to-all(f32[64,16,1]{0,2,1:T(1,128)S(1)} %bitcast.34), channel_id=1, replica_groups=mesh['expert'=16,'replica'=2] {'expert'}, dimensions={1} | all-to-all | bytes 8192 | tf_op jit(solution)/shard_map/all_to_all | solution.py:60
  322.7 12.5 %multiply_convert_fusion = bf16[1024,3584]{1,0:T(8,128)(2,1)} fusion(bf16[1024,1024]{1,0:T(8,128)(2,1)} %all-gather.2.cloned.1.call-done, bf16[1,1024,3584]{2,1,0:T(8,128)(2,1)} %param.11, f32[1024]{0:T(1024)S(1)} %mul.31), kind=kOutput, calls=%fused_computation | convolution fusion | flops 7530872832 | bytes 16781312 | tf_op jit(solution)/shard_map/dot_general | solution.py:75
  335.2 160.0 %reduce-scatter.5.cloned.1.call-done = bf16[64,3584]{1,0:T(8,128)(2,1)} async-done(((bf16[1024,3584]{1,0:T(8,128)(2,1)}), bf16[64,3584]{1,0:T(8,128)(2,1)}) %reduce-scatter.5.cloned.1.call-update) | async-done | bytes 458768 | tf_op jit(solution)/shard_map/reduce_scatter | solution.py:81
  (71 shorter events, 2.0 us)
Async XLA Ops:
  6.5 300.1 %reduce-scatter.3.cloned.1.call-start = ((), (), s32[]{:S(2)}) async-start(), calls=%async_computation.3 | async-start | bytes 12582912 | tf_op jit(solution)/shard_map/reduce_scatter | solution.py:73
  6.5 12.5 %collective-permute-start = (bf16[64,3584]{1,0:T(8,128)(2,1)}, bf16[64,3584]{1,0:T(8,128)(2,1)S(1)}, u32[]{:S(2)}, u32[]{:S(2)}) collective-permute-start(bf16[64,3584]{1,0:T(8,128)(2,1)} %param.6), channel_id=1, source_target_pairs={{0,2},{2,4},{4,6},{6,8},{8,10},{10,12},{12,14},{14,16},{16,18},{18... | collective-permute-start | bytes 1376264 | tf_op jit(solution)/shard_map/ppermute | solution.py:63
  19.0 12.0 %collective-permute-start.1 = (bf16[64,3584]{1,0:T(8,128)(2,1)S(1)}, bf16[64,3584]{1,0:T(8,128)(2,1)S(1)}, u32[]{:S(2)}, u32[]{:S(2)}) collective-permute-start(bf16[64,3584]{1,0:T(8,128)(2,1)S(1)} %collective-permute-done), channel_id=1, source_target_pairs={{0,2},{2,4},{4,6},{6,8},{8,10},{10,12},{12,14},{14,16},{16,18},{18... | collective-permute-start | bytes 1376264 | tf_op jit(solution)/shard_map/ppermute | solution.py:63
  31.0 12.3 %collective-permute-start.2 = (bf16[64,3584]{1,0:T(8,128)(2,1)S(1)}, bf16[64,3584]{1,0:T(8,128)(2,1)S(1)}, u32[]{:S(2)}, u32[]{:S(2)}) collective-permute-start(bf16[64,3584]{1,0:T(8,128)(2,1)S(1)} %collective-permute-done.1), channel_id=1, source_target_pairs={{0,2},{2,4},{4,6},{6,8},{8,10},{10,12},{12,14},{14,16},{16,18},{18... | collective-permute-start | bytes 1376264 | tf_op jit(solution)/shard_map/ppermute | solution.py:63
  43.3 11.5 %collective-permute-start.3 = (bf16[64,3584]{1,0:T(8,128)(2,1)S(1)}, bf16[64,3584]{1,0:T(8,128)(2,1)S(1)}, u32[]{:S(2)}, u32[]{:S(2)}) collective-permute-start(bf16[64,3584]{1,0:T(8,128)(2,1)S(1)} %collective-permute-done.2), channel_id=1, source_target_pairs={{0,2},{2,4},{4,6},{6,8},{8,10},{10,12},{12,14},{14,16},{16,18},{18... | collective-permute-start | bytes 1376264 | tf_op jit(solution)/shard_map/ppermute | solution.py:63
  54.8 10.7 %collective-permute-start.4 = (bf16[64,3584]{1,0:T(8,128)(2,1)S(1)}, bf16[64,3584]{1,0:T(8,128)(2,1)S(1)}, u32[]{:S(2)}, u32[]{:S(2)}) collective-permute-start(bf16[64,3584]{1,0:T(8,128)(2,1)S(1)} %collective-permute-done.3), channel_id=1, source_target_pairs={{0,2},{2,4},{4,6},{6,8},{8,10},{10,12},{12,14},{14,16},{16,18},{18... | collective-permute-start | bytes 1376264 | tf_op jit(solution)/shard_map/ppermute | solution.py:63
  65.5 10.9 %collective-permute-start.5 = (bf16[64,3584]{1,0:T(8,128)(2,1)S(1)}, bf16[64,3584]{1,0:T(8,128)(2,1)S(1)}, u32[]{:S(2)}, u32[]{:S(2)}) collective-permute-start(bf16[64,3584]{1,0:T(8,128)(2,1)S(1)} %collective-permute-done.4), channel_id=1, source_target_pairs={{0,2},{2,4},{4,6},{6,8},{8,10},{10,12},{12,14},{14,16},{16,18},{18... | collective-permute-start | bytes 1376264 | tf_op jit(solution)/shard_map/ppermute | solution.py:63
  76.4 11.8 %collective-permute-start.6 = (bf16[64,3584]{1,0:T(8,128)(2,1)S(1)}, bf16[64,3584]{1,0:T(8,128)(2,1)S(1)}, u32[]{:S(2)}, u32[]{:S(2)}) collective-permute-start(bf16[64,3584]{1,0:T(8,128)(2,1)S(1)} %collective-permute-done.5), channel_id=1, source_target_pairs={{0,2},{2,4},{4,6},{6,8},{8,10},{10,12},{12,14},{14,16},{16,18},{18... | collective-permute-start | bytes 1376264 | tf_op jit(solution)/shard_map/ppermute | solution.py:63
  88.2 0.8 copy-start.2
  89.1 13.0 %collective-permute-start.7 = (bf16[64,3584]{1,0:T(8,128)(2,1)S(1)}, bf16[64,3584]{1,0:T(8,128)(2,1)S(1)}, u32[]{:S(2)}, u32[]{:S(2)}) collective-permute-start(bf16[64,3584]{1,0:T(8,128)(2,1)S(1)} %collective-permute-done.6), channel_id=1, source_target_pairs={{0,2},{2,4},{4,6},{6,8},{8,10},{10,12},{12,14},{14,16},{16,18},{18... | collective-permute-start | bytes 1376264 | tf_op jit(solution)/shard_map/ppermute | solution.py:63
  102.0 0.8 copy-start.4
  102.8 14.1 %collective-permute-start.8 = (bf16[64,3584]{1,0:T(8,128)(2,1)S(1)}, bf16[64,3584]{1,0:T(8,128)(2,1)S(1)}, u32[]{:S(2)}, u32[]{:S(2)}) collective-permute-start(bf16[64,3584]{1,0:T(8,128)(2,1)S(1)} %collective-permute-done.7), channel_id=1, source_target_pairs={{0,2},{2,4},{4,6},{6,8},{8,10},{10,12},{12,14},{14,16},{16,18},{18... | collective-permute-start | bytes 1376264 | tf_op jit(solution)/shard_map/ppermute | solution.py:63
  117.0 0.8 copy-start.6
  117.7 15.3 %collective-permute-start.9 = (bf16[64,3584]{1,0:T(8,128)(2,1)S(1)}, bf16[64,3584]{1,0:T(8,128)(2,1)S(1)}, u32[]{:S(2)}, u32[]{:S(2)}) collective-permute-start(bf16[64,3584]{1,0:T(8,128)(2,1)S(1)} %collective-permute-done.8), channel_id=1, source_target_pairs={{0,2},{2,4},{4,6},{6,8},{8,10},{10,12},{12,14},{14,16},{16,18},{18... | collective-permute-start | bytes 1376264 | tf_op jit(solution)/shard_map/ppermute | solution.py:63
  133.1 0.8 copy-start.8
  133.8 14.6 %collective-permute-start.10 = (bf16[64,3584]{1,0:T(8,128)(2,1)S(1)}, bf16[64,3584]{1,0:T(8,128)(2,1)S(1)}, u32[]{:S(2)}, u32[]{:S(2)}) collective-permute-start(bf16[64,3584]{1,0:T(8,128)(2,1)S(1)} %collective-permute-done.9), channel_id=1, source_target_pairs={{0,2},{2,4},{4,6},{6,8},{8,10},{10,12},{12,14},{14,16},{16,18},{18... | collective-permute-start | bytes 1376264 | tf_op jit(solution)/shard_map/ppermute | solution.py:63
  148.4 0.8 copy-start.10
  149.2 13.4 %collective-permute-start.11 = (bf16[64,3584]{1,0:T(8,128)(2,1)S(1)}, bf16[64,3584]{1,0:T(8,128)(2,1)S(1)}, u32[]{:S(2)}, u32[]{:S(2)}) collective-permute-start(bf16[64,3584]{1,0:T(8,128)(2,1)S(1)} %collective-permute-done.10), channel_id=1, source_target_pairs={{0,2},{2,4},{4,6},{6,8},{8,10},{10,12},{12,14},{14,16},{16,18},{18... | collective-permute-start | bytes 1376264 | tf_op jit(solution)/shard_map/ppermute | solution.py:63
  162.6 0.8 copy-start.12
  163.4 12.5 %collective-permute-start.12 = (bf16[64,3584]{1,0:T(8,128)(2,1)S(1)}, bf16[64,3584]{1,0:T(8,128)(2,1)S(1)}, u32[]{:S(2)}, u32[]{:S(2)}) collective-permute-start(bf16[64,3584]{1,0:T(8,128)(2,1)S(1)} %collective-permute-done.11), channel_id=1, source_target_pairs={{0,2},{2,4},{4,6},{6,8},{8,10},{10,12},{12,14},{14,16},{16,18},{18... | collective-permute-start | bytes 1376264 | tf_op jit(solution)/shard_map/ppermute | solution.py:63
  175.9 0.8 copy-start.13
  176.7 13.4 %collective-permute-start.13 = (bf16[64,3584]{1,0:T(8,128)(2,1)S(1)}, bf16[64,3584]{1,0:T(8,128)(2,1)}, u32[]{:S(2)}, u32[]{:S(2)}) collective-permute-start(bf16[64,3584]{1,0:T(8,128)(2,1)S(1)} %collective-permute-done.12), channel_id=1, source_target_pairs={{0,2},{2,4},{4,6},{6,8},{8,10},{10,12},{12,14},{14,16},{16,18},{18... | collective-permute-start | bytes 1376264 | tf_op jit(solution)/shard_map/ppermute | solution.py:63
  190.0 34.9 %collective-permute-start.14 = (bf16[64,3584]{1,0:T(8,128)(2,1)}, bf16[64,3584]{1,0:T(8,128)(2,1)}, u32[]{:S(2)}, u32[]{:S(2)}) collective-permute-start(bf16[64,3584]{1,0:T(8,128)(2,1)} %collective-permute-done.13), channel_id=1, source_target_pairs={{0,2},{2,4},{4,6},{6,8},{8,10},{10,12},{12,14},{14,16},{16,18},{18... | collective-permute-start | bytes 1376264 | tf_op jit(solution)/shard_map/ppermute | solution.py:63
  206.1 30.1 %copy-start.1 = (bf16[64,3584]{1,0:T(8,128)(2,1)S(1)}, bf16[64,3584]{1,0:T(8,128)(2,1)}, u32[]{:S(2)}) copy-start(bf16[64,3584]{1,0:T(8,128)(2,1)} %param.6) | copy-start | bytes 1376260
  224.9 15.6 %copy-start.11 = (bf16[64,3584]{1,0:T(8,128)(2,1)S(1)}, bf16[64,3584]{1,0:T(8,128)(2,1)}, u32[]{:S(2)}) copy-start(bf16[64,3584]{1,0:T(8,128)(2,1)} %copy-done.10) | copy-start | bytes 1376260
  224.9 15.7 %copy-start.9 = (bf16[64,3584]{1,0:T(8,128)(2,1)S(1)}, bf16[64,3584]{1,0:T(8,128)(2,1)}, u32[]{:S(2)}) copy-start(bf16[64,3584]{1,0:T(8,128)(2,1)} %copy-done.8) | copy-start | bytes 1376260
  224.9 15.7 %copy-start.7 = (bf16[64,3584]{1,0:T(8,128)(2,1)S(1)}, bf16[64,3584]{1,0:T(8,128)(2,1)}, u32[]{:S(2)}) copy-start(bf16[64,3584]{1,0:T(8,128)(2,1)} %copy-done.6) | copy-start | bytes 1376260
  224.9 15.8 %copy-start.5 = (bf16[64,3584]{1,0:T(8,128)(2,1)S(1)}, bf16[64,3584]{1,0:T(8,128)(2,1)}, u32[]{:S(2)}) copy-start(bf16[64,3584]{1,0:T(8,128)(2,1)} %copy-done.4) | copy-start | bytes 1376260
  224.9 15.8 %copy-start.3 = (bf16[64,3584]{1,0:T(8,128)(2,1)S(1)}, bf16[64,3584]{1,0:T(8,128)(2,1)}, u32[]{:S(2)}) copy-start(bf16[64,3584]{1,0:T(8,128)(2,1)} %copy-done.2) | copy-start | bytes 1376260
  224.9 21.3 %copy-start = (bf16[2048,3584]{1,0:T(8,128)(2,1)S(1)}, bf16[2048,3584]{1,0:T(8,128)(2,1)}, u32[]{:S(2)}) copy-start(bf16[2048,3584]{1,0:T(8,128)(2,1)} %copy.16) | copy-start | bytes 44040196
  241.0 5.1 %copy-start.15 = (bf16[2048,3584]{1,0:T(8,128)(2,1)}, bf16[2048,3584]{1,0:T(8,128)(2,1)S(1)}, u32[]{:S(2)}) copy-start(bf16[2048,3584]{1,0:T(8,128)(2,1)S(1)} %constant_dynamic-update-slice_fusion) | copy-start | bytes 44040196
  265.5 45.1 %copy-start.14 = (f32[64,8]{0,1:T(8,128)S(1)}, f32[64,8]{0,1:T(8,128)}, u32[]{:S(2)}) copy-start(f32[64,8]{0,1:T(8,128)} %param.8) | copy-start | bytes 6148
  265.5 45.1 %copy-start.16 = (s32[64,8]{0,1:T(8,128)S(1)}, s32[64,8]{0,1:T(8,128)}, u32[]{:S(2)}) copy-start(s32[64,8]{0,1:T(8,128)} %param.7) | copy-start | bytes 6148
  265.5 45.1 %copy-start.17 = (s32[16]{0:T(128)S(1)}, s32[16]{0:T(128)}, u32[]{:S(2)}) copy-start(s32[16]{0:T(128)} %param.9) | copy-start | bytes 196
  265.5 57.2 %all-gather.2.cloned.1.call-start = ((), (), s32[]{:S(2)}) async-start(), calls=%async_computation.4 | async-start | bytes 3145728 | tf_op jit(solution)/shard_map/all_gather | solution.py:76
  310.5 184.7 %reduce-scatter.5.cloned.1.call-start = ((), (), s32[]{:S(2)}) async-start(), calls=%async_computation.5 | async-start | bytes 7798784 | tf_op jit(solution)/shard_map/reduce_scatter | solution.py:81
Sparse Core Ops, SparseCore 0:
  265.6 40.9 reduce-scatter.2
  310.6 11.7 all-gather.1
  335.3 159.8 reduce-scatter.4
